TPU v7x, 32 devices: a whole 2x2x4 slice. The times are simulated.
32 devices in a mesh: grp: 1, freq: 32 (over z, y, x, core), pair: 1.
Axes of the slice: x: 2, y: 2, z: 4, core: 2. Of those that a mesh axis runs over, the one named last changes fastest.
Arguments:
- spectra: bfloat16 [96, 1024, 2, 512], P(('grp', 'pair'), 'freq'), may hold values from -6 to 6
- valid: int32 [96, 512], P(('grp', 'pair')), may hold values 0 or 1
- ref_spectra: bfloat16 [96, 1024, 2, 256], P(('grp', 'pair'), 'freq'), may hold values from -6 to 6
- ref_valid: int32 [96, 256], P(('grp', 'pair')), may hold values 0 or 1
Outputs:
- xcorr: float32 [401, 512, 256], P('grp', ('freq', 'pair'))
All inputs are finite; a program needn't handle non-finite values. No bound on the sum of `valid` or of `ref_valid` on one device may be relied on, other than what follows from the above.
Results may differ from a plain program's by a relative error of at most 0.0054.
Values may be sent and summed in bfloat16 or wider, within the bound.
A program may use at most 192 MiB of HBM per device.

v0:
```python
import jax
import jax.numpy as jnp
from jax import lax
from jax.sharding import PartitionSpec as P

F = 1024
LAGS = 401
REACH = 10


water_level = 0.1


def with_halo(array, sides, width):
    for axis, dim in sides:
        count, length = (lax.axis_size(axis), array.shape[dim])
        up = [(i, (i + 1) % count) for i in range(count - 1)]
        down = [(j, i) for i, j in up]
        last = lax.slice_in_dim(array, length - width, length, axis=dim)
        first = lax.slice_in_dim(array, 0, width, axis=dim)
        before = lax.ppermute(last, axis, up)
        after = lax.ppermute(first, axis, down)
        array = jnp.concatenate([before, array, after], axis=dim)
    return array


def power_of(spectra):
    real_part = spectra[:, :, 0].astype(jnp.float32)
    imag_part = spectra[:, :, 1].astype(jnp.float32)
    return real_part * real_part + imag_part * imag_part


def lag_table(bin_total):
    bin_index = jnp.arange(bin_total, dtype=jnp.int32)
    offsets = jnp.arange(LAGS, dtype=jnp.int32) - (LAGS - 1) // 2
    phases = jnp.mod(offsets[:, None] * bin_index[None, :], F).astype(jnp.float32) * (
        2.0 * jnp.pi / F
    )
    norm_scale = 1.0 / jnp.sqrt(jnp.float32(F))
    return jnp.stack([jnp.cos(phases) * norm_scale, -jnp.sin(phases) * norm_scale], axis=1).astype(
        jnp.bfloat16
    )


def rotated(white):
    turned = jnp.stack([-white[:, :, 1], white[:, :, 0]], axis=2)
    return jnp.concatenate([white, turned], axis=3)


def local(spectra, valid, ref_spectra, ref_valid):
    local_bins = spectra.shape[1]
    stations = spectra.shape[3]
    sources = ref_spectra.shape[3]
    freq_devs = lax.axis_size("freq")
    pair_devs = lax.axis_size("pair")
    recv_local = stations // (freq_devs * pair_devs)
    powers = jnp.concatenate([power_of(spectra), power_of(ref_spectra)], axis=2)
    padded = with_halo(powers, (("freq", 1),), REACH)
    out_bins = jnp.arange(local_bins, dtype=jnp.int32)[:, None]
    in_bins = jnp.arange(local_bins + 2 * REACH, dtype=jnp.int32)[None, :]
    band_ones = jnp.where(
        (in_bins >= out_bins) & (in_bins <= out_bins + 2 * REACH), 1.0, 0.0
    ).astype(jnp.float32)
    smooth = jnp.einsum("wks,fk->wfs", padded, band_ones, precision=lax.Precision.HIGHEST) / (
        2 * REACH + 1
    )
    inverse_amp = lax.rsqrt(smooth + water_level)
    rec_gain = inverse_amp[:, :, :stations] * valid.astype(jnp.float32)[:, None, :]
    ref_gain = inverse_amp[:, :, stations:] * ref_valid.astype(jnp.float32)[:, None, :]
    rec_white = (spectra.astype(jnp.float32) * rec_gain[:, :, None, :]).astype(jnp.bfloat16)
    ref_white = (ref_spectra.astype(jnp.float32) * ref_gain[:, :, None, :]).astype(jnp.bfloat16)
    ref_both = rotated(ref_white)
    cross_gram = jnp.einsum(
        "wfcj,wfck->fjk", rec_white, ref_both, preferred_element_type=jnp.float32
    )
    pair_count = jnp.dot(
        valid.astype(jnp.float32).T, ref_valid.astype(jnp.float32), precision=lax.Precision.HIGHEST
    )
    cross_gram = cross_gram.reshape(local_bins, freq_devs, pair_devs, recv_local, 2, sources)
    pair_count = pair_count.reshape(1, freq_devs, pair_devs, recv_local, 1, sources)
    cross_gram, pair_count = (
        lax.psum_scatter(cross_gram, "pair", scatter_dimension=2, tiled=True),
        lax.psum_scatter(pair_count, "pair", scatter_dimension=2, tiled=True),
    )
    cross_gram = cross_gram.reshape(local_bins, freq_devs, recv_local, 2, sources)
    pair_count = pair_count.reshape(1, freq_devs, recv_local, 1, sources)
    stacked = (cross_gram / jnp.sqrt(pair_count + 1.0)).astype(jnp.bfloat16)
    lag_weights = lag_table(F)
    return jnp.einsum(
        "fxrcs,lcf->lrs",
        lax.all_to_all(stacked, "freq", split_axis=1, concat_axis=0, tiled=True),
        lag_weights,
        preferred_element_type=jnp.float32,
    )


def solution(mesh):
    placed = (
        P(("grp", "pair"), "freq", None, None),
        P(("grp", "pair"), None),
        P(("grp", "pair"), "freq", None, None),
        P(("grp", "pair"), None),
    )
    return jax.shard_map(
        local,
        mesh=mesh,
        in_specs=placed,
        out_specs=P("grp", ("freq", "pair"), None),
        check_vma=False,
    )
```

profile of v0, /device:TPU:0, one launch (start us, length us, event | category | flops | bytes accessed | tf_op | source)
XLA Modules:
  0.0 636.2 jit_solution(3155681868966570516)
XLA Ops:
  0.0 14.1 %fusion.41 = (bf16[96,32,1,512]{3,2,1,0:T(2,128)(2,1)S(1)}, bf16[96,32,1,512]{3,2,1,0:T(2,128)(2,1)}) fusion(bf16[96,32,2,512]{3,2,1,0:T(2,128)(2,1)} %param.4), kind=kLoop, calls=%fused_computation.63 | loop fusion | bytes 12582912 | tf_op jit(solution)/shard_map/slice | solution.py:28
  14.1 7.8 %fusion.42 = (bf16[96,32,1,256]{3,2,1,0:T(2,128)(2,1)}, bf16[96,32,1,256]{3,2,1,0:T(2,128)(2,1)}) fusion(bf16[96,32,2,256]{3,2,1,0:T(2,128)(2,1)S(1)} %copy-done), kind=kLoop, calls=%fused_computation.64 | loop fusion | bytes 6291456 | tf_op jit(solution)/shard_map/slice | solution.py:28
  22.0 4.7 add_bitcast_fusion
  26.7 3.9 add_bitcast_fusion.1
  33.7 2.7 collective-permute-start
  41.3 4.0 copy.48
  45.3 2.0 collective-permute-done.1
  47.3 4.0 copy.49
  51.3 18.3 %rsqrt_bitcast_fusion = f32[96,32,768]{2,1,0:T(8,128)} fusion(f32[96,10,768]{2,1,0:T(8,128)} %copy.49, f32[96,32,256]{2,1,0:T(8,128)S(1)} %add_bitcast_fusion.1, f32[96,32,512]{2,1,0:T(8,128)S(1)} %add_bitcast_fusion, f32[96,10,768]{2,1,0:T(8,128)} %copy.48, s32[32]{0:T(128)S(1)} %iota_add_fusion.1), kind=kOutput, calls=%fused_computation.14 | convolution fusion | flops 1488427520 | bytes 24772736 | tf_op jit(solution)/shard_map/wks,fk->wfs/dot_general | solution.py:64
  69.6 2.3 slice_multiply_fusion.1
  72.0 1.8 copy.51
  73.8 3.6 multiply_convert_fusion.1
  79.3 4.4 slice_multiply_fusion
  83.7 7.6 %multiply_convert_fusion = bf16[96,32,2,512]{3,2,1,0:T(2,128)(2,1)} fusion(bf16[96,32,2,512]{3,2,1,0:T(2,128)(2,1)S(1)} %bitcast.25, f32[96,32,512]{2,1,0:T(8,128)S(1)} %slice_multiply_fusion), kind=kLoop, calls=%fused_computation.11 | loop fusion | flops 9437184 | bytes 18874368 | tf_op jit(solution)/shard_map/convert_element_type | solution.py:70
  91.3 19.4 %convolution_bitcast_fusion = f32[32,512,512]{2,1,0:T(8,128)} fusion(bf16[96,32,1,256]{3,0,2,1:T(8,128)(2,1)} %get-tuple-element.10, bf16[96,32,1,256]{3,0,2,1:T(8,128)(2,1)} %get-tuple-element.9, bf16[96,32,2,256]{3,0,2,1:T(8,128)(2,1)S(1)} %multiply_convert_fusion.1, bf16[96,32,2,512]{3,2,1,0:T(2,128)(2,1)} %multiply_convert_fusion), kind=kOutput, calls=%fused_computation.10 | convolution fusion | flops 3240099840 | bytes 46137344 | tf_op jit(solution)/shard_map/wfcj,wfck->fjk/dot_general | solution.py:73
  110.7 38.7 %reshape.147 = f32[32,32,16,2,256]{4,3,2,1,0:T(2,128)} reshape(f32[32,512,512]{2,1,0:T(8,128)} %convolution_bitcast_fusion) | data formatting | bytes 67108864 | tf_op jit(solution)/shard_map/reshape | solution.py:85
  149.4 16.5 %fusion = bf16[32,32,16,2,256]{4,2,3,1,0:T(8,128)(2,1)S(1)} fusion(f32[32,32,16,2,256]{4,3,2,1,0:T(2,128)} %reshape.147, f32[32,16,256]{2,1,0:T(8,128)S(1)} %bitcast.27), kind=kLoop, calls=%fused_computation.1 | loop fusion | flops 16777216 | bytes 50855936 | tf_op jit(solution)/shard_map/convert_element_type | solution.py:87
  165.8 11.4 %copy.54 = bf16[32,32,16,2,256]{4,3,2,0,1:T(2,128)(2,1)} copy(bf16[32,32,16,2,256]{4,2,3,1,0:T(8,128)(2,1)S(1)} %fusion) | data formatting | bytes 33554432 | tf_op jit(solution)/shard_map/convert_element_type | solution.py:87
  177.3 64.3 %all-to-all-start = ((bf16[32,32,16,2,256]{4,3,2,0,1:T(2,128)(2,1)}), bf16[32,32,16,2,256]{4,3,2,0,1:T(2,128)(2,1)}, u32[]{:S(2)}, u32[]{:S(2)}) async-start(bf16[32,32,16,2,256]{4,3,2,0,1:T(2,128)(2,1)} %copy.54), calls=%async_computation | async-start | bytes 33554432 | tf_op jit(solution)/shard_map/all_to_all | solution.py:91
  241.6 7.0 %multiply_convert_fusion.3 = (bf16[401,1,1024]{2,0,1:T(8,128)(2,1)S(1)}, bf16[401,1,1024]{2,0,1:T(8,128)(2,1)S(1)}) fusion(s32[401]{0:T(512)S(1)} %iota_add_fusion), kind=kLoop, calls=%fused_computation.39 | loop fusion | flops 7801856 | bytes 1644100 | tf_op jit(solution)/shard_map/convert
  248.6 365.5 %all-to-all-done = bf16[32,32,16,2,256]{4,3,2,0,1:T(2,128)(2,1)} async-done(((bf16[32,32,16,2,256]{4,3,2,0,1:T(2,128)(2,1)}), bf16[32,32,16,2,256]{4,3,2,0,1:T(2,128)(2,1)}, u32[]{:S(2)}, u32[]{:S(2)}) %all-to-all-start) | async-done | bytes 16777248 | tf_op jit(solution)/shard_map/all_to_all | solution.py:91
  614.1 10.1 %copy.55 = bf16[32,32,1,16,2,256]{5,1,0,4,3,2:T(8,128)(2,1)S(1)} copy(bf16[32,32,1,16,2,256]{5,4,3,1,0,2:T(2,128)(2,1)} %bitcast.9) | data formatting | bytes 33554432 | tf_op jit(solution)/shard_map/all_to_all | solution.py:91
  624.2 7.0 %convolution_bitcast_fusion.1 = f32[401,16,256]{2,0,1:T(8,128)S(1)} fusion(bf16[1024,16,2,256]{3,0,2,1:T(8,128)(2,1)S(1)} %bitcast.26, bf16[401,1,1024]{2,0,1:T(8,128)(2,1)S(1)} %get-tuple-element.14, bf16[401,1,1024]{2,0,1:T(8,128)(2,1)S(1)} %get-tuple-element.13), kind=kOutput, calls=%fused_computation.28 | convolution fusion | flops 6730948608 | bytes 24989696 | tf_op jit(solution)/shard_map/fxrcs,lcf->lrs/dot_general | solution.py:89
  631.2 4.8 copy.56
  (24 shorter events, 9.7 us)
Async XLA Ops:
  0.0 14.1 %copy-start = (bf16[96,32,2,256]{3,2,1,0:T(2,128)(2,1)S(1)}, bf16[96,32,2,256]{3,2,1,0:T(2,128)(2,1)}, u32[]{:S(2)}) copy-start(bf16[96,32,2,256]{3,2,1,0:T(2,128)(2,1)} %param.6) | copy-start | bytes 9437188
  33.7 6.0 copy-start.3
  33.7 6.0 copy-start.2
  33.7 7.6 %collective-permute-start = (f32[96,10,768]{2,0,1:T(8,128)S(1)}, f32[96,10,768]{2,0,1:T(8,128)S(1)}, u32[]{:S(2)}, u32[]{:S(2)}) collective-permute-start(f32[96,10,768]{2,0,1:T(8,128)S(1)} %copy.46), channel_id=1, source_target_pairs={{0,1},{1,2},{2,3},{3,4},{4,5},{5,6},{6,7},{7,8},{8,9},{9,10},{10,1... | collective-permute-start | bytes 8847368 | tf_op jit(solution)/shard_map/ppermute | solution.py:21
  38.1 9.2 %collective-permute-start.1 = (f32[96,10,768]{2,0,1:T(8,128)S(1)}, f32[96,10,768]{2,0,1:T(8,128)S(1)}, u32[]{:S(2)}, u32[]{:S(2)}) collective-permute-start(f32[96,10,768]{2,0,1:T(8,128)S(1)} %copy.47), channel_id=1, source_target_pairs={{1,0},{2,1},{3,2},{4,3},{5,4},{6,5},{7,6},{8,7},{9,8},{10,9},{11,1... | collective-permute-start | bytes 8847368 | tf_op jit(solution)/shard_map/ppermute | solution.py:22
  77.4 6.2 slice-start
  79.3 4.4 slice-start.1
  110.7 38.7 %copy-start.1 = (f32[512,256]{1,0:T(8,128)S(1)}, f32[512,256]{1,0:T(8,128)}, u32[]{:S(2)}) copy-start(f32[512,256]{1,0:T(8,128)} %fusion.26) | copy-start | bytes 1572868
  177.3 436.8 %all-to-all-start = ((bf16[32,32,16,2,256]{4,3,2,0,1:T(2,128)(2,1)}), bf16[32,32,16,2,256]{4,3,2,0,1:T(2,128)(2,1)}, u32[]{:S(2)}, u32[]{:S(2)}) async-start(bf16[32,32,16,2,256]{4,3,2,0,1:T(2,128)(2,1)} %copy.54), calls=%async_computation | async-start | bytes 33554432 | tf_op jit(solution)/shard_map/all_to_all | solution.py:91
where the time goes:
time: 645 us; the launch traced here: 636 us
  waiting for transfers between devices  367 us (57%)
  local copies, waits for them, and re-layouts  100 us (16%)
  starting transfers between devices  68.5 us (11%)
  other arithmetic  53.3 us (8%)
  matrix products  46.3 us (7%)
    all_to_all x1, waiting for transfers between devices, local(): lax.all_to_all(stacked, 'freq', split_axis=1, concat_axis=0, tiled=True)  365 us
    all_to_all x1, starting transfers between devices, local(): lax.all_to_all(stacked, 'freq', split_axis=1, concat_axis=0, tiled=True)  64.3 us
    reshape x1, local copies, waits for them, and re-layouts, local(): cross_gram.reshape(local_bins, freq_devs, recv_local, 2, sources)  38.7 us
    slice x2, local copies, waits for them, and re-layouts, power_of(): real_part = spectra[:, :, 0].astype(jnp.float32)  22 us
    dot_general x1, matrix products, local(): jnp.einsum('wfcj,wfck->fjk', rec_white, ref_both, preferred_element_type=...  19.4 us
    dot_general x1, matrix products, local(): jnp.einsum('wks,fk->wfs', padded, band_ones, precision=lax.Precision.HIGH...  18.3 us
    convert_element_type x1, other arithmetic, local(): stacked = (cross_gram / jnp.sqrt(pair_count + 1.0)).astype(jnp.bfloat16)  16.5 us
  transfers between devices with their start and end apart: 3, of which 2 were waited for; matrix products, arithmetic and copies ran while one was open for 2% of the time, Pallas kernels for 0%

commit v1 on v0

--- a/solution.py
+++ b/solution.py
@@ -1,6 +1,11 @@
+import functools
+import math
+
 import jax
 import jax.numpy as jnp
 from jax import lax
+from jax.experimental import pallas as pl
+from jax.experimental.pallas import tpu as pltpu
 from jax.sharding import PartitionSpec as P
 
 F = 1024
@@ -30,16 +35,132 @@
     return real_part * real_part + imag_part * imag_part
 
 
-def lag_table(bin_total):
-    bin_index = jnp.arange(bin_total, dtype=jnp.int32)
-    offsets = jnp.arange(LAGS, dtype=jnp.int32) - (LAGS - 1) // 2
-    phases = jnp.mod(offsets[:, None] * bin_index[None, :], F).astype(jnp.float32) * (
-        2.0 * jnp.pi / F
-    )
+def half_table(first_bin, bins, devs, rows):
+    column = lax.broadcasted_iota(jnp.int32, (rows, devs * 2 * bins), 1)
+    lag = lax.broadcasted_iota(jnp.int32, (rows, devs * 2 * bins), 0) - (LAGS - 1) // 2
+    bin_index = first_bin + column // (2 * bins) * bins + column % bins
+    imag = column // bins % 2
+    phases = jnp.mod(lag * bin_index, F).astype(jnp.float32) * (2.0 * jnp.pi / F)
     norm_scale = 1.0 / jnp.sqrt(jnp.float32(F))
-    return jnp.stack([jnp.cos(phases) * norm_scale, -jnp.sin(phases) * norm_scale], axis=1).astype(
-        jnp.bfloat16
-    )
+    values = jnp.where(imag == 1, -jnp.sin(phases), jnp.cos(phases)) * norm_scale
+    return values.astype(jnp.bfloat16)
+
+
+def exchange_kernel(n, chunks, x_ref, w_ref, out_ref, buf, part, got, send_sem, recv_sem, part_sem, got_sem, own_sem):
+    h = n // 2
+    rows_chunk = x_ref.shape[1] // chunks
+    depth = h * x_ref.shape[2]
+    sources = x_ref.shape[3]
+    lags = out_ref.shape[1]
+    me = lax.axis_index("freq")
+    half = lax.div(me, h)
+    pos = lax.rem(me, h)
+    base = half * h
+    other = (1 - half) * h
+    partner = other + pos
+
+    barrier = pltpu.get_barrier_semaphore()
+
+    @pl.loop(1, h)
+    def _(k):
+        pl.semaphore_signal(barrier, inc=1, device_id={"freq": base + lax.rem(pos + k, h)}, device_id_type=pl.DeviceIdType.MESH)
+
+    pl.semaphore_signal(barrier, inc=1, device_id={"freq": partner}, device_id_type=pl.DeviceIdType.MESH)
+    pl.semaphore_wait(barrier, h)
+
+    def bins_copy(s, c, k):
+        p = lax.rem(pos + k, h)
+        rows = pl.ds(c * rows_chunk, rows_chunk)
+        return pltpu.make_async_remote_copy(
+            src_ref=x_ref.at[(other if s == 0 else base) + p, rows],
+            dst_ref=buf.at[s, rows, pos],
+            send_sem=send_sem.at[s, c, k],
+            recv_sem=recv_sem.at[s, c, k],
+            device_id={"freq": base + p},
+            device_id_type=pl.DeviceIdType.MESH,
+        )
+
+    def own_copy(s):
+        return pltpu.make_async_copy(x_ref.at[(other if s == 0 else base) + pos], buf.at[s, :, pos], own_sem.at[s])
+
+    def sums_copy(c):
+        rows = pl.ds(c * rows_chunk, rows_chunk)
+        return pltpu.make_async_remote_copy(
+            src_ref=part.at[rows],
+            dst_ref=got.at[rows],
+            send_sem=part_sem.at[c],
+            recv_sem=got_sem.at[c],
+            device_id={"freq": partner},
+            device_id_type=pl.DeviceIdType.MESH,
+        )
+
+    def send_bins(s, c):
+        @pl.loop(1, h)
+        def _(k):
+            bins_copy(s, c, k).start()
+
+    def wait_bins(s, c):
+        @pl.loop(1, h)
+        def _(k):
+            bins_copy(s, c, k).wait_recv()
+
+    def to_lags(s, j):
+        return jnp.dot(w_ref[...], buf[s, j].reshape(depth, sources), preferred_element_type=jnp.float32)
+
+    own_copy(0).start()
+    own_copy(1).start()
+    for c in range(chunks):
+        send_bins(0, c)
+    own_copy(0).wait()
+    for c in range(chunks):
+        wait_bins(0, c)
+
+        @pl.loop(c * rows_chunk, (c + 1) * rows_chunk)
+        def _(j):
+            part[j] = to_lags(0, j).astype(jnp.bfloat16)
+
+        sums_copy(c).start()
+        send_bins(1, c)
+    own_copy(1).wait()
+    for c in range(chunks):
+        wait_bins(1, c)
+        sums_copy(c).wait_recv()
+
+        @pl.loop(c * rows_chunk, (c + 1) * rows_chunk)
+        def _(j):
+            total = to_lags(1, j) + got[j].astype(jnp.float32)
+            out_ref[j] = total[:lags]
+
+    for c in range(chunks):
+        sums_copy(c).wait_send()
+        for s in range(2):
+            @pl.loop(1, h)
+            def _(k):
+                bins_copy(s, c, k).wait_send()
+
+
+def exchange(stacked, weights):
+    n, recv_local, depth, sources = stacked.shape
+    rows = weights.shape[0]
+    h = n // 2
+    chunks = math.gcd(recv_local, 4)
+    return pl.pallas_call(
+        functools.partial(exchange_kernel, n, chunks),
+        out_shape=jax.ShapeDtypeStruct((recv_local, LAGS, sources), jnp.float32),
+        in_specs=[pl.BlockSpec(memory_space=pl.ANY), pl.BlockSpec(memory_space=pltpu.VMEM)],
+        out_specs=pl.BlockSpec(memory_space=pltpu.VMEM),
+        scratch_shapes=[
+            pltpu.VMEM((2, recv_local, h, depth, sources), jnp.bfloat16),
+            pltpu.VMEM((recv_local, rows, sources), jnp.bfloat16),
+            pltpu.VMEM((recv_local, rows, sources), jnp.bfloat16),
+            pltpu.SemaphoreType.DMA((2, chunks, h)),
+            pltpu.SemaphoreType.DMA((2, chunks, h)),
+            pltpu.SemaphoreType.DMA((chunks,)),
+            pltpu.SemaphoreType.DMA((chunks,)),
+            pltpu.SemaphoreType.DMA((2,)),
+        ],
+        compiler_params=pltpu.CompilerParams(collective_id=0, has_side_effects=True, vmem_limit_bytes=56 * 1024 * 1024),
+    )(stacked, weights)
 
 
 def rotated(white):
@@ -76,22 +197,24 @@
     pair_count = jnp.dot(
         valid.astype(jnp.float32).T, ref_valid.astype(jnp.float32), precision=lax.Precision.HIGHEST
     )
-    cross_gram = cross_gram.reshape(local_bins, freq_devs, pair_devs, recv_local, 2, sources)
-    pair_count = pair_count.reshape(1, freq_devs, pair_devs, recv_local, 1, sources)
-    cross_gram, pair_count = (
-        lax.psum_scatter(cross_gram, "pair", scatter_dimension=2, tiled=True),
-        lax.psum_scatter(pair_count, "pair", scatter_dimension=2, tiled=True),
-    )
-    cross_gram = cross_gram.reshape(local_bins, freq_devs, recv_local, 2, sources)
-    pair_count = pair_count.reshape(1, freq_devs, recv_local, 1, sources)
-    stacked = (cross_gram / jnp.sqrt(pair_count + 1.0)).astype(jnp.bfloat16)
-    lag_weights = lag_table(F)
-    return jnp.einsum(
-        "fxrcs,lcf->lrs",
-        lax.all_to_all(stacked, "freq", split_axis=1, concat_axis=0, tiled=True),
-        lag_weights,
-        preferred_element_type=jnp.float32,
-    )
+    if pair_devs > 1:
+        cross_gram = cross_gram.reshape(local_bins, freq_devs, pair_devs, recv_local, 2 * sources)
+        pair_count = pair_count.reshape(1, freq_devs, pair_devs, recv_local, sources)
+        cross_gram, pair_count = (
+            lax.psum_scatter(cross_gram, "pair", scatter_dimension=2, tiled=True),
+            lax.psum_scatter(pair_count, "pair", scatter_dimension=2, tiled=True),
+        )
+    cross_gram = cross_gram.reshape(local_bins, freq_devs * recv_local, 2 * sources)
+    pair_count = pair_count.reshape(freq_devs * recv_local, sources)
+    norm = jnp.sqrt(pair_count + 1.0)
+    norm = jnp.concatenate([norm, norm], axis=1)
+    stacked = (cross_gram / norm[None]).astype(jnp.bfloat16)
+    stacked = jnp.stack([stacked[:, :, :sources], stacked[:, :, sources:]], axis=0)
+    stacked = stacked.transpose(2, 0, 1, 3).reshape(freq_devs, recv_local, 2 * local_bins, sources)
+    half_devs = freq_devs // 2
+    first_bin = lax.axis_index("freq") // half_devs * (half_devs * local_bins)
+    weights = half_table(first_bin, local_bins, half_devs, -(-LAGS // 16) * 16)
+    return exchange(stacked, weights).transpose(1, 0, 2)
 
 
 def solution(mesh):

time: 645 us -> 516 us (0.80)
  the two profiles are of different devices: /device:TPU:0 before, /device:TPU:15 now
where the time goes in v1:
time: 516 us; the launch traced here: 509 us
  Pallas kernels  322 us (62%)
  local copies, waits for them, and re-layouts  86.7 us (17%)
  other arithmetic  39.4 us (8%)
  matrix products  37.8 us (7%)
  waiting for transfers between devices  16.4 us (3%)
  starting transfers between devices  5.88 us (1%)
    pallas_call x1, Pallas kernels, exchange(): pl.pallas_call(functools.partial(exchange_kernel, n, chunks), out_shape=j...  322 us
    transpose x1, local copies, waits for them, and re-layouts, local(): stacked.transpose(2, 0, 1, 3)  26.4 us
    slice x2, local copies, waits for them, and re-layouts, power_of(): real_part = spectra[:, :, 0].astype(jnp.float32)  19.3 us
    dot_general x1, matrix products, local(): jnp.einsum('wks,fk->wfs', padded, band_ones, precision=lax.Precision.HIGH...  18.3 us
    dot_general x1, matrix products, local(): jnp.einsum('wfcj,wfck->fjk', rec_white, ref_both, preferred_element_type=...  17.8 us
    ppermute x1, waiting for transfers between devices, with_halo(): before = lax.ppermute(last, axis, up)  12.9 us
  transfers between devices with their start and end apart: 2, of which 2 were waited for; matrix products, arithmetic and copies ran while one was open for 5% of the time, Pallas kernels for 0%

profile of v1, /device:TPU:15, one launch (start us, length us, event | category | flops | bytes accessed | tf_op | source)
XLA Modules:
  0.0 509.0 jit_solution(15545975670917289649)
XLA Ops:
  0.0 13.9 %fusion.45 = (bf16[96,32,1,512]{3,2,1,0:T(2,128)(2,1)S(1)}, bf16[96,32,1,512]{3,2,1,0:T(2,128)(2,1)}) fusion(bf16[96,32,2,512]{3,2,1,0:T(2,128)(2,1)} %param.4), kind=kLoop, calls=%fused_computation.79 | loop fusion | bytes 12582912 | tf_op jit(solution)/shard_map/slice | solution.py:33
  14.0 5.3 %fusion.46 = (bf16[96,32,1,256]{3,2,1,0:T(2,128)(2,1)S(1)}, bf16[96,32,1,256]{3,2,1,0:T(2,128)(2,1)}) fusion(bf16[96,32,2,256]{3,2,1,0:T(2,128)(2,1)S(1)} %copy-done), kind=kLoop, calls=%fused_computation.80 | loop fusion | bytes 6291456 | tf_op jit(solution)/shard_map/slice | solution.py:33
  19.3 4.7 add_bitcast_fusion
  24.0 5.0 add_bitcast_fusion.1
  30.8 3.3 copy.19
  34.1 3.8 collective-permute-start
  37.9 3.4 copy.20
  41.2 2.1 collective-permute-start.1
  46.8 2.5 copy.26
  49.4 8.0 %multiply_convert_fusion.2.w_ref = bf16[416,1024]{1,0:T(8,128)(2,1)} fusion(s32[1024]{0:T(1024)S(1)} %get-tuple-element.16, s32[1024]{0:T(1024)S(1)} %get-tuple-element.18, s32[1024]{0:T(1024)S(1)} %get-tuple-element.17, s32[1024]{0:T(1024)S(1)} %get-tuple-element.21, s32[]{:T(128)S(6)} %mul.82, s32[416]{0:T(512)S(1)} %iota_add_fusion, ...), kind=kLoop, calls=%fused_computation.43 | loop fusion | flops 15335424 | bytes 881284 | tf_op jit(solution)/shard_map/convert_element_type | solution.py:46
  57.4 12.9 %collective-permute-done = f32[96,10,768]{2,0,1:T(8,128)} collective-permute-done((f32[96,10,768]{2,0,1:T(8,128)}, f32[96,10,768]{2,0,1:T(8,128)}, u32[]{:S(2)}, u32[]{:S(2)}) %collective-permute-start) | collective-permute-done | bytes 2949152 | tf_op jit(solution)/shard_map/ppermute | solution.py:26
  70.3 6.0 %copy.21 = f32[96,10,768]{2,1,0:T(8,128)} copy(f32[96,10,768]{2,0,1:T(8,128)} %collective-permute-done) | data formatting | bytes 5898240 | tf_op jit(solution)/shard_map/ppermute | solution.py:26
  76.3 3.6 collective-permute-done.1
  79.9 5.8 %copy.22 = f32[96,10,768]{2,1,0:T(8,128)} copy(f32[96,10,768]{2,0,1:T(8,128)} %collective-permute-done.1) | data formatting | bytes 5898240 | tf_op jit(solution)/shard_map/ppermute | solution.py:27
  85.7 18.3 %rsqrt_bitcast_fusion = f32[96,32,768]{2,1,0:T(8,128)} fusion(f32[96,10,768]{2,1,0:T(8,128)} %copy.22, f32[96,32,256]{2,1,0:T(8,128)S(1)} %copy-done.3, f32[96,32,512]{2,1,0:T(8,128)S(1)} %bitcast.27, f32[96,10,768]{2,1,0:T(8,128)} %copy.21, s32[32]{0:T(128)S(1)} %iota_add_fusion.1), kind=kOutput, calls=%fused_computation.14 | convolution fusion | flops 1488427520 | bytes 24772736 | tf_op jit(solution)/shard_map/wks,fk->wfs/dot_general | solution.py:185
  104.1 2.3 slice_multiply_fusion.1
  108.3 4.0 multiply_convert_fusion.1
  113.9 1.9 slice_negate_fusion
  118.1 7.5 %multiply_convert_fusion = bf16[96,32,2,512]{3,2,1,0:T(2,128)(2,1)} fusion(bf16[96,32,2,512]{3,2,1,0:T(2,128)(2,1)S(1)} %bitcast.24, f32[96,32,512]{2,1,0:T(8,128)S(1)} %slice_multiply_fusion), kind=kLoop, calls=%fused_computation.11 | loop fusion | flops 9437184 | bytes 18874368 | tf_op jit(solution)/shard_map/convert_element_type | solution.py:191
  125.7 17.8 %fusion = bf16[32,512,512]{2,1,0:T(8,128)(2,1)} fusion(f32[512,512]{1,0:T(8,128)} %copy.26, bf16[96,32,1,256]{3,0,2,1:T(8,128)(2,1)} %get-tuple-element.12, bf16[96,32,1,256]{3,0,2,1:T(8,128)(2,1)} %get-tuple-element.11, bf16[96,32,2,256]{3,0,2,1:T(8,128)(2,1)S(1)} %copy-done.5, bf16[96,32,2,512]{3,2,1,0:T(2,128)(2,1)} %multiply_convert_fusion), kind=kOutput, calls=%fused_computation.1 | convolution fusion | flops 3256877056 | bytes 30408704 | tf_op jit(solution)/shard_map/wfcj,wfck->fjk/dot_general | solution.py:194
  143.5 7.1 %slice_bitcast_fusion.1 = (bf16[1,32,512,256]{3,2,1,0:T(8,128)(2,1)S(1)}, bf16[1,32,512,256]{3,2,1,0:T(8,128)(2,1)S(1)}) fusion(bf16[32,512,512]{2,1,0:T(8,128)(2,1)} %fusion), kind=kLoop, calls=%fused_computation.16 | loop fusion | bytes 33554432 | tf_op jit(solution)/shard_map/stack | solution.py:212
  152.2 26.4 %copy.27 = bf16[512,2,32,256]{3,2,1,0:T(8,128)(2,1)} copy(bf16[512,2,32,256]{3,0,2,1:T(8,128)(2,1)S(1)} %maximum_bitcast_fusion) | data formatting | bytes 33554432 | tf_op jit(solution)/shard_map/transpose | solution.py:213
  178.6 322.1 %shard_map.46 = f32[16,401,256]{2,1,0:T(8,128)} custom-call(bf16[32,16,64,256]{3,2,1,0:T(8,128)(2,1)} %bitcast.22, bf16[416,1024]{1,0:T(8,128)(2,1)} %multiply_convert_fusion.2.w_ref), custom_call_target="tpu_custom_call" | custom-call | tf_op jit(solution)/shard_map/pallas_call | solution.py:147
  500.7 7.8 %copy.28 = f32[401,16,256]{2,1,0:T(8,128)} copy(f32[401,16,256]{2,0,1:T(8,128)} %bitcast.25) | data formatting | bytes 13139968 | tf_op jit(solution)/shard_map/transpose | solution.py:217
  (50 shorter events, 12.8 us)
Async XLA Ops:
  0.0 14.0 %copy-start = (bf16[96,32,2,256]{3,2,1,0:T(2,128)(2,1)S(1)}, bf16[96,32,2,256]{3,2,1,0:T(2,128)(2,1)}, u32[]{:S(2)}) copy-start(bf16[96,32,2,256]{3,2,1,0:T(2,128)(2,1)} %param.6) | copy-start | bytes 9437188
  24.0 5.0 copy-start.1
  29.0 1.8 copy-start.2
  34.1 9.3 %copy-start.7 = (s32[96,256]{1,0:T(8,128)S(1)}, s32[96,256]{1,0:T(8,128)}, u32[]{:S(2)}) copy-start(s32[96,256]{1,0:T(8,128)} %param.7) | copy-start | bytes 294916
  34.1 9.9 %copy-start.6 = (s32[96,512]{1,0:T(8,128)S(1)}, s32[96,512]{1,0:T(8,128)}, u32[]{:S(2)}) copy-start(s32[96,512]{1,0:T(8,128)} %param.5) | copy-start | bytes 589828
  34.1 36.3 %collective-permute-start = (f32[96,10,768]{2,0,1:T(8,128)}, f32[96,10,768]{2,0,1:T(8,128)}, u32[]{:S(2)}, u32[]{:S(2)}) collective-permute-start(f32[96,10,768]{2,0,1:T(8,128)} %copy.19), channel_id=1, source_target_pairs={{0,1},{1,2},{2,3},{3,4},{4,5},{5,6},{6,7},{7,8},{8,9},{9,10},{10,1... | collective-permute-start | bytes 8847368 | tf_op jit(solution)/shard_map/ppermute | solution.py:26
  41.2 38.7 %collective-permute-start.1 = (f32[96,10,768]{2,0,1:T(8,128)}, f32[96,10,768]{2,0,1:T(8,128)}, u32[]{:S(2)}, u32[]{:S(2)}) collective-permute-start(f32[96,10,768]{2,0,1:T(8,128)} %copy.20), channel_id=1, source_target_pairs={{1,0},{2,1},{3,2},{4,3},{5,4},{6,5},{7,6},{8,7},{9,8},{10,9},{11,1... | collective-permute-start | bytes 8847368 | tf_op jit(solution)/shard_map/ppermute | solution.py:27
  70.3 15.4 %slice-start.2 = ((s8[6291456]{0:T(1024)(128)(4,1)}), s8[4194304]{0:T(1024)(128)(4,1)S(1)}, s32[]{:S(2)}) async-start(s8[6291456]{0:T(1024)(128)(4,1)} %bitcast.26), calls=%async_computation.2 | async-start | bytes 8388608
  76.3 9.4 %slice-start.3 = ((s8[6291456]{0:T(1024)(128)(4,1)}), s8[2097152]{0:T(1024)(128)(4,1)S(1)}, s32[]{:S(2)}) async-start(s8[6291456]{0:T(1024)(128)(4,1)} %bitcast.26), calls=%async_computation.3 | async-start | bytes 4194304
  76.3 9.4 %copy-start.3 = (f32[96,32,256]{2,1,0:T(8,128)S(1)}, f32[96,32,256]{2,1,0:T(8,128)}, u32[]{:S(2)}) copy-start(f32[96,32,256]{2,1,0:T(8,128)} %copy-done.2) | copy-start | bytes 9437188
  85.7 18.3 %copy-start.8 = (f32[96,256]{1,0:T(8,128)S(1)}, f32[96,256]{1,0:T(8,128)}, u32[]{:S(2)}) copy-start(f32[96,256]{1,0:T(8,128)} %convert_element_type.53) | copy-start | bytes 294916
  106.4 9.4 %slice-start.4 = ((s8[9437184]{0:T(1024)(128)(4,1)}), s8[4194304]{0:T(1024)(128)(4,1)S(1)}, s32[]{:S(2)}) async-start(s8[9437184]{0:T(1024)(128)(4,1)} %bitcast.28), calls=%async_computation.4 | async-start | bytes 8388608
  108.3 7.5 %slice-start.5 = ((s8[9437184]{0:T(1024)(128)(4,1)}), s8[4194304]{0:T(1024)(128)(4,1)S(1)}, s32[]{:S(2)}) async-start(s8[9437184]{0:T(1024)(128)(4,1)} %bitcast.28), calls=%async_computation.5 | async-start | bytes 8388608
  108.3 7.5 %slice-start.6 = ((s8[9437184]{0:T(1024)(128)(4,1)}), s8[1048576]{0:T(1024)(128)(4,1)S(1)}, s32[]{:S(2)}) async-start(s8[9437184]{0:T(1024)(128)(4,1)} %bitcast.28), calls=%async_computation.6 | async-start | bytes 2097152
  112.2 1.7 copy-start.4
  113.9 3.3 slice-start
  115.8 2.3 slice-start.1
  118.1 7.5 %copy-start.5 = (bf16[96,32,2,256]{3,0,2,1:T(8,128)(2,1)S(1)}, bf16[96,32,2,256]{3,0,2,1:T(8,128)(2,1)}, u32[]{:S(2)}) copy-start(bf16[96,32,2,256]{3,0,2,1:T(8,128)(2,1)} %copy-done.4) | copy-start | bytes 9437188

commit v2 on v1

--- a/solution.py
+++ b/solution.py
@@ -11,28 +11,117 @@
 F = 1024
 LAGS = 401
 REACH = 10
+LANES = 128
 
 
 water_level = 0.1
 
 
-def with_halo(array, sides, width):
-    for axis, dim in sides:
-        count, length = (lax.axis_size(axis), array.shape[dim])
-        up = [(i, (i + 1) % count) for i in range(count - 1)]
-        down = [(j, i) for i, j in up]
-        last = lax.slice_in_dim(array, length - width, length, axis=dim)
-        first = lax.slice_in_dim(array, 0, width, axis=dim)
-        before = lax.ppermute(last, axis, up)
-        after = lax.ppermute(first, axis, down)
-        array = jnp.concatenate([before, array, after], axis=dim)
-    return array
-
-
-def power_of(spectra):
-    real_part = spectra[:, :, 0].astype(jnp.float32)
-    imag_part = spectra[:, :, 1].astype(jnp.float32)
-    return real_part * real_part + imag_part * imag_part
+def edge_powers(spectra, ref_spectra, first, width):
+    parts = []
+    for array in (spectra, ref_spectra):
+        edge = lax.slice_in_dim(array, first, first + width, axis=1).transpose(1, 2, 0, 3).astype(jnp.float32)
+        parts.append(edge[:, 0] * edge[:, 0] + edge[:, 1] * edge[:, 1])
+    return jnp.concatenate(parts, axis=2)
+
+
+def halo_powers(spectra, ref_spectra, axis):
+    count, length = lax.axis_size(axis), spectra.shape[1]
+    up = [(i, (i + 1) % count) for i in range(count - 1)]
+    down = [(j, i) for i, j in up]
+    last = edge_powers(spectra, ref_spectra, length - REACH, REACH)
+    first = edge_powers(spectra, ref_spectra, 0, REACH)
+    return lax.ppermute(last, axis, up), lax.ppermute(first, axis, down)
+
+
+def gram_kernel(x_ref, y_ref, before_ref, after_ref, valid_ref, ref_valid_ref, scale_ref, out_ref, power, gram, sem):
+    bins = x_ref.shape[0]
+    stations = x_ref.shape[3]
+    sources = y_ref.shape[3]
+    block = out_ref.shape[2]
+    step = pl.program_id(0)
+
+    @pl.when(step == 0)
+    def _():
+        copies = (
+            pltpu.make_async_copy(before_ref, power.at[pl.ds(0, REACH)], sem.at[0]),
+            pltpu.make_async_copy(after_ref, power.at[pl.ds(REACH + bins, REACH)], sem.at[1]),
+        )
+        for copy in copies:
+            copy.start()
+
+        @pl.loop(0, bins)
+        def _(f):
+            for ref, columns in ((x_ref, pl.ds(0, stations)), (y_ref, pl.ds(stations, sources))):
+                real_part = ref[f, 0].astype(jnp.float32)
+                imag_part = ref[f, 1].astype(jnp.float32)
+                power[f + REACH, :, columns] = real_part * real_part + imag_part * imag_part
+
+        for copy in copies:
+            copy.wait()
+
+        @pl.loop(0, bins + 2 * REACH - 2)
+        def _(f):
+            power[f] = power[f] + power[f + 1] + power[f + 2]
+
+    @pl.loop(0, block)
+    def _(b):
+        f = step * block + b
+        whites = []
+        for ref, mask, columns in (
+            (x_ref, valid_ref, pl.ds(0, stations)),
+            (y_ref, ref_valid_ref, pl.ds(stations, sources)),
+        ):
+            smooth = power[f, :, columns]
+            for k in range(3, 2 * REACH + 1, 3):
+                smooth = smooth + power[f + k, :, columns]
+            gain = lax.rsqrt(smooth * (1.0 / (2 * REACH + 1)) + water_level) * mask[...]
+            whites.append([ref[f, c].astype(jnp.float32) * gain for c in range(2)])
+        (rec_re, rec_im), (ref_re, ref_im) = whites
+        rec = jnp.concatenate([rec_re.astype(jnp.bfloat16), rec_im.astype(jnp.bfloat16)], axis=0)
+        for c, pieces in enumerate(((ref_re, ref_im), (-ref_im, ref_re))):
+            other = jnp.concatenate([piece.astype(jnp.bfloat16) for piece in pieces], axis=0)
+            cross = lax.dot_general(rec, other, (((0,), (0,)), ((), ())), preferred_element_type=jnp.float32)
+            cross = cross * scale_ref[...]
+            for q in range(sources // LANES):
+                gram[c * (sources // LANES) + q, pl.ds(pl.multiple_of(b * stations, stations), stations)] = cross[
+                    :, q * LANES : (q + 1) * LANES
+                ]
+
+    @pl.loop(0, stations, unroll=8)
+    def _(j):
+        for c in range(2):
+            for q in range(sources // LANES):
+                rows = gram[c * (sources // LANES) + q, pl.ds(j, block, stride=stations)]
+                out_ref[j, c, :, pl.ds(q * LANES, LANES)] = rows.astype(out_ref.dtype)
+
+
+def cross_grams(spectra, ref_spectra, before, after, valid, ref_valid, scale, dtype):
+    bins, parts, windows, stations = spectra.shape
+    sources = ref_spectra.shape[3]
+    block = 8
+    whole = lambda shape: pl.BlockSpec(shape, lambda i: (0,) * len(shape), pipeline_mode=pl.Buffered(1))
+    return pl.pallas_call(
+        gram_kernel,
+        grid=(bins // block,),
+        out_shape=jax.ShapeDtypeStruct((stations, 2, bins, sources), dtype),
+        in_specs=[
+            whole(spectra.shape),
+            whole(ref_spectra.shape),
+            pl.BlockSpec(memory_space=pl.ANY),
+            pl.BlockSpec(memory_space=pl.ANY),
+            whole(valid.shape),
+            whole(ref_valid.shape),
+            whole(scale.shape),
+        ],
+        out_specs=pl.BlockSpec((stations, 2, block, sources), lambda i: (0, 0, i, 0)),
+        scratch_shapes=[
+            pltpu.VMEM((bins + 2 * REACH, windows, stations + sources), jnp.float32),
+            pltpu.VMEM((2 * sources // LANES, block * stations, LANES), jnp.float32),
+            pltpu.SemaphoreType.DMA((2,)),
+        ],
+        compiler_params=pltpu.CompilerParams(vmem_limit_bytes=60 * 1024 * 1024),
+    )(spectra, ref_spectra, before, after, valid, ref_valid, scale)
 
 
 def half_table(first_bin, bins, devs, rows):
@@ -163,11 +252,6 @@
     )(stacked, weights)
 
 
-def rotated(white):
-    turned = jnp.stack([-white[:, :, 1], white[:, :, 0]], axis=2)
-    return jnp.concatenate([white, turned], axis=3)
-
-
 def local(spectra, valid, ref_spectra, ref_valid):
     local_bins = spectra.shape[1]
     stations = spectra.shape[3]
@@ -175,42 +259,26 @@
     freq_devs = lax.axis_size("freq")
     pair_devs = lax.axis_size("pair")
     recv_local = stations // (freq_devs * pair_devs)
-    powers = jnp.concatenate([power_of(spectra), power_of(ref_spectra)], axis=2)
-    padded = with_halo(powers, (("freq", 1),), REACH)
-    out_bins = jnp.arange(local_bins, dtype=jnp.int32)[:, None]
-    in_bins = jnp.arange(local_bins + 2 * REACH, dtype=jnp.int32)[None, :]
-    band_ones = jnp.where(
-        (in_bins >= out_bins) & (in_bins <= out_bins + 2 * REACH), 1.0, 0.0
-    ).astype(jnp.float32)
-    smooth = jnp.einsum("wks,fk->wfs", padded, band_ones, precision=lax.Precision.HIGHEST) / (
-        2 * REACH + 1
-    )
-    inverse_amp = lax.rsqrt(smooth + water_level)
-    rec_gain = inverse_amp[:, :, :stations] * valid.astype(jnp.float32)[:, None, :]
-    ref_gain = inverse_amp[:, :, stations:] * ref_valid.astype(jnp.float32)[:, None, :]
-    rec_white = (spectra.astype(jnp.float32) * rec_gain[:, :, None, :]).astype(jnp.bfloat16)
-    ref_white = (ref_spectra.astype(jnp.float32) * ref_gain[:, :, None, :]).astype(jnp.bfloat16)
-    ref_both = rotated(ref_white)
-    cross_gram = jnp.einsum(
-        "wfcj,wfck->fjk", rec_white, ref_both, preferred_element_type=jnp.float32
-    )
-    pair_count = jnp.dot(
-        valid.astype(jnp.float32).T, ref_valid.astype(jnp.float32), precision=lax.Precision.HIGHEST
+    before, after = halo_powers(spectra, ref_spectra, "freq")
+    valid = valid.astype(jnp.float32)
+    ref_valid = ref_valid.astype(jnp.float32)
+    pair_count = jnp.dot(valid.T, ref_valid, precision=lax.Precision.HIGHEST)
+    if pair_devs == 1:
+        scale, dtype = 1.0 / jnp.sqrt(pair_count + 1.0), jnp.bfloat16
+    else:
+        scale, dtype = jnp.ones_like(pair_count), jnp.float32
+    stacked = cross_grams(
+        spectra.transpose(1, 2, 0, 3), ref_spectra.transpose(1, 2, 0, 3), before, after, valid, ref_valid, scale, dtype
     )
     if pair_devs > 1:
-        cross_gram = cross_gram.reshape(local_bins, freq_devs, pair_devs, recv_local, 2 * sources)
-        pair_count = pair_count.reshape(1, freq_devs, pair_devs, recv_local, sources)
-        cross_gram, pair_count = (
-            lax.psum_scatter(cross_gram, "pair", scatter_dimension=2, tiled=True),
-            lax.psum_scatter(pair_count, "pair", scatter_dimension=2, tiled=True),
+        stacked = stacked.reshape(freq_devs, pair_devs, recv_local, 2 * local_bins, sources)
+        pair_count = pair_count.reshape(freq_devs, pair_devs, recv_local, 1, sources)
+        stacked, pair_count = (
+            lax.psum_scatter(stacked, "pair", scatter_dimension=1, tiled=True),
+            lax.psum_scatter(pair_count, "pair", scatter_dimension=1, tiled=True),
         )
-    cross_gram = cross_gram.reshape(local_bins, freq_devs * recv_local, 2 * sources)
-    pair_count = pair_count.reshape(freq_devs * recv_local, sources)
-    norm = jnp.sqrt(pair_count + 1.0)
-    norm = jnp.concatenate([norm, norm], axis=1)
-    stacked = (cross_gram / norm[None]).astype(jnp.bfloat16)
-    stacked = jnp.stack([stacked[:, :, :sources], stacked[:, :, sources:]], axis=0)
-    stacked = stacked.transpose(2, 0, 1, 3).reshape(freq_devs, recv_local, 2 * local_bins, sources)
+        stacked = (stacked / jnp.sqrt(pair_count + 1.0)).astype(jnp.bfloat16)
+    stacked = stacked.reshape(freq_devs, recv_local, 2 * local_bins, sources)
     half_devs = freq_devs // 2
     first_bin = lax.axis_index("freq") // half_devs * (half_devs * local_bins)
     weights = half_table(first_bin, local_bins, half_devs, -(-LAGS // 16) * 16)

time: 516 us -> 428 us (0.83); the launches traced: 509 us -> 428 us
  local copies, waits for them, and re-layouts: 86.7 us -> 26.3 us
  Pallas kernels: 322 us -> 364 us
  matrix products: 37.8 us -> 1.44 us
  other arithmetic: 39.4 us -> 16 us
    pallas_call x0 -> x1, Pallas kernels: none -> 46 us  [cross_grams(): pl.pallas_call(gram_kernel, grid=(bins // block,), out_shape=jax.ShapeDty...]
    dot_general x3 -> x1, matrix products: 37.8 us -> 1.44 us  [local(): pair_count = jnp.dot(valid.T, ref_valid, precision=lax.Precision.HIGHEST)]
    transpose x1 -> x0, local copies, waits for them, and re-layouts: 26.4 us -> none  [local(): stacked.transpose(2, 0, 1, 3)]
    slice x4 -> x2, local copies, waits for them, and re-layouts: 25.9 us -> 5.52 us  [edge_powers(): lax.slice_in_dim(array, first, first + width, axis=1).transpose(1, 2, 0, 3)]
    ppermute x2 -> x0, local copies, waits for them, and re-layouts: 11.8 us -> none  [the longest x1 6.03 us: with_halo(): before = lax.ppermute(last, axis, up)]
    unnamed x32 -> x14, local copies, waits for them, and re-layouts: 3.33 us -> 13 us
    convert_element_type x4, other arithmetic: 12.2 us -> 3.1 us  [the longest x2 1.75 us: edge_powers(): lax.slice_in_dim(array, first, first + width, axis=1).transpose(1, 2, 0, 3)]
    add x3 -> x4, other arithmetic: 9.69 us -> 1.19 us  [edge_powers(): parts.append(edge[:, 0] * edge[:, 0] + edge[:, 1] * edge[:, 1])]
  transfers between devices with their start and end apart: 2 -> 2, of which waited for: 2 -> 2; matrix products, arithmetic and copies ran while one was open for 5% -> 6% of each run, Pallas kernels for 0% -> 0%
where the time goes in v2:
time: 428 us
  Pallas kernels  364 us (85%)
  local copies, waits for them, and re-layouts  26.3 us (6%)
  other arithmetic  16 us (4%)
  waiting for transfers between devices  13.6 us (3%)
  starting transfers between devices  5.76 us (1%)
    pallas_call x1, Pallas kernels, exchange(): pl.pallas_call(functools.partial(exchange_kernel, n, chunks), out_shape=j...  318 us
    pallas_call x1, Pallas kernels, cross_grams(): pl.pallas_call(gram_kernel, grid=(bins // block,), out_shape=jax.ShapeDty...  46 us
    ppermute x2, waiting for transfers between devices, halo_powers(): return (lax.ppermute(last, axis, up), lax.ppermute(first, axis, down))  13.6 us
    unnamed x14, local copies, waits for them, and re-layouts  13 us
  transfers between devices with their start and end apart: 2, of which 2 were waited for; matrix products, arithmetic and copies ran while one was open for 6% of the time, Pallas kernels for 0%

profile of v2, /device:TPU:15, one launch (start us, length us, event | category | flops | bytes accessed | tf_op | source)
XLA Modules:
  0.0 427.6 jit_solution(4225170601918702019)
XLA Ops:
  0.0 2.7 fusion.25
  2.8 0.5 convert_bitcast_fusion.2
  3.3 0.1 fusion.13
  3.4 0.9 slice-done.1
  4.4 2.8 fusion.24
  7.1 1.2 convert_bitcast_fusion
  8.4 0.5 fusion.3
  8.9 1.8 pad_maximum_fusion
  10.7 3.7 collective-permute-start
  14.4 0.1 fusion.11
  14.5 0.5 fusion.1
  15.0 1.8 pad_maximum_fusion.1
  16.8 2.1 collective-permute-start.1
  18.9 7.8 %copy.22 = bf16[96,32,2,512]{3,0,2,1:T(8,128)(2,1)} copy(bf16[96,32,2,512]{3,2,1,0:T(2,128)(2,1)S(1)} %bitcast.28) | data formatting | bytes 12582912 | tf_op args[0]
  26.8 4.2 copy.23
  31.0 0.7 convert_element_type.44.valid_ref
  31.7 0.6 convert_element_type.45.ref_valid_ref
  32.4 1.4 fusion.9.scale_ref
  33.9 8.0 %multiply_convert_fusion.w_ref = bf16[416,1024]{1,0:T(8,128)(2,1)} fusion(s32[1024]{0:T(1024)S(1)} %get-tuple-element.14, s32[1024]{0:T(1024)S(1)} %get-tuple-element.16, s32[1024]{0:T(1024)S(1)} %get-tuple-element.15, s32[1024]{0:T(1024)S(1)} %get-tuple-element.19, s32[]{:T(128)S(6)} %mul.62, s32[416]{0:T(512)S(1)} %iota_add_fusion, ...), kind=kLoop, calls=%fused_computation.29 | loop fusion | flops 15335424 | bytes 881284 | tf_op jit(solution)/shard_map/convert_element_type | solution.py:135
  41.9 4.9 %collective-permute-done.before_ref = f32[10,96,768]{2,1,0:T(8,128)S(1)} collective-permute-done((f32[10,96,768]{2,1,0:T(8,128)}, f32[10,96,768]{2,1,0:T(8,128)S(1)}, u32[]{:S(2)}, u32[]{:S(2)}) %collective-permute-start) | collective-permute-done | bytes 2949152 | tf_op jit(solution)/shard_map/ppermute | solution.py:34
  46.8 8.7 %collective-permute-done.1.after_ref = f32[10,96,768]{2,1,0:T(8,128)} collective-permute-done((f32[10,96,768]{2,1,0:T(8,128)}, f32[10,96,768]{2,1,0:T(8,128)}, u32[]{:S(2)}, u32[]{:S(2)}) %collective-permute-start.1) | collective-permute-done | bytes 2949152 | tf_op jit(solution)/shard_map/ppermute | solution.py:34
  55.5 46.0 %shard_map.46 = bf16[512,2,32,256]{3,2,1,0:T(8,128)(2,1)} custom-call(bf16[32,2,96,512]{3,2,1,0:T(8,128)(2,1)} %bitcast.26, bf16[32,2,96,256]{3,2,1,0:T(8,128)(2,1)} %bitcast.29, f32[10,96,768]{2,1,0:T(8,128)} %copy-done.1, f32[10,96,768]{2,1,0:T(8,128)} %collective-permute-done.1.after_ref, f32[96,512]{1,0:T(8,128)} %convert_element_type.44.valid_ref, ...), custom_call_target="tpu_custom_call" | custom-call | tf_op jit(solution)/shard_map/pallas_call | solution.py:104
  101.5 318.3 %shard_map.47 = f32[16,401,256]{2,1,0:T(8,128)} custom-call(bf16[32,16,64,256]{3,2,1,0:T(8,128)(2,1)} %bitcast.24, bf16[416,1024]{1,0:T(8,128)(2,1)} %multiply_convert_fusion.w_ref), custom_call_target="tpu_custom_call" | custom-call | tf_op jit(solution)/shard_map/pallas_call | solution.py:236
  419.8 7.8 %copy.11 = f32[401,16,256]{2,1,0:T(8,128)} copy(f32[401,16,256]{2,0,1:T(8,128)} %bitcast.25) | data formatting | bytes 13139968 | tf_op jit(solution)/shard_map/transpose | solution.py:285
  (18 shorter events, 0.1 us)
Async XLA Ops:
  0.0 3.4 slice-start
  2.7 1.6 slice-start.1
  10.7 36.1 %collective-permute-start = (f32[10,96,768]{2,1,0:T(8,128)}, f32[10,96,768]{2,1,0:T(8,128)S(1)}, u32[]{:S(2)}, u32[]{:S(2)}) collective-permute-start(f32[10,96,768]{2,1,0:T(8,128)} %pad_maximum_fusion), channel_id=1, source_target_pairs={{0,1},{1,2},{2,3},{3,4},{4,5},{5,6},{6,7},{7,8},{8,9},{9,10},{10,1... | collective-permute-start | bytes 8847368 | tf_op jit(solution)/shard_map/ppermute | solution.py:34
  16.8 38.7 %collective-permute-start.1 = (f32[10,96,768]{2,1,0:T(8,128)}, f32[10,96,768]{2,1,0:T(8,128)}, u32[]{:S(2)}, u32[]{:S(2)}) collective-permute-start(f32[10,96,768]{2,1,0:T(8,128)} %pad_maximum_fusion.1), channel_id=1, source_target_pairs={{1,0},{2,1},{3,2},{4,3},{5,4},{6,5},{7,6},{8,7},{9,8},{10,9},{11,1... | collective-permute-start | bytes 8847368 | tf_op jit(solution)/shard_map/ppermute | solution.py:34
  18.9 7.9 %copy-start = (bf16[96,32,2,256]{3,2,1,0:T(2,128)(2,1)S(1)}, bf16[96,32,2,256]{3,2,1,0:T(2,128)(2,1)}, u32[]{:S(2)}) copy-start(bf16[96,32,2,256]{3,2,1,0:T(2,128)(2,1)} %param.6) | copy-start | bytes 9437188
  26.8 4.2 copy-start.2
  26.8 4.9 %copy-start.3 = (s32[96,256]{1,0:T(8,128)S(1)}, s32[96,256]{1,0:T(8,128)}, u32[]{:S(2)}) copy-start(s32[96,256]{1,0:T(8,128)} %param.7) | copy-start | bytes 294916
  46.8 8.7 %copy-start.1 = (f32[10,96,768]{2,1,0:T(8,128)}, f32[10,96,768]{2,1,0:T(8,128)S(1)}, u32[]{:S(2)}) copy-start(f32[10,96,768]{2,1,0:T(8,128)S(1)} %collective-permute-done.before_ref) | copy-start | bytes 8847364

commit v3 on v2

--- a/solution.py
+++ b/solution.py
@@ -12,6 +12,7 @@
 LAGS = 401
 REACH = 10
 LANES = 128
+LAG_ROWS = 16
 
 
 water_level = 0.1
@@ -124,18 +125,22 @@
     )(spectra, ref_spectra, before, after, valid, ref_valid, scale)
 
 
-def half_table(first_bin, bins, devs, rows):
-    column = lax.broadcasted_iota(jnp.int32, (rows, devs * 2 * bins), 1)
-    lag = lax.broadcasted_iota(jnp.int32, (rows, devs * 2 * bins), 0) - (LAGS - 1) // 2
-    bin_index = first_bin + column // (2 * bins) * bins + column % bins
-    imag = column // bins % 2
-    phases = jnp.mod(lag * bin_index, F).astype(jnp.float32) * (2.0 * jnp.pi / F)
-    norm_scale = 1.0 / jnp.sqrt(jnp.float32(F))
-    values = jnp.where(imag == 1, -jnp.sin(phases), jnp.cos(phases)) * norm_scale
+def lag_rows(first_lag, first_bin, bins, shape):
+    column = lax.broadcasted_iota(jnp.int32, shape, 1)
+    lag = lax.broadcasted_iota(jnp.int32, shape, 0) + first_lag + (F - (LAGS - 1) // 2)
+    bin_index = first_bin + lax.div(column, 2 * bins) * bins + lax.rem(column, bins)
+    imag = lax.rem(lax.div(column, bins), 2)
+    phases = lax.rem(lag * bin_index, F).astype(jnp.float32) * (2.0 * jnp.pi / F)
+    values = jnp.where(imag == 1, -jnp.sin(phases), jnp.cos(phases)) * (1.0 / math.sqrt(F))
     return values.astype(jnp.bfloat16)
 
 
-def exchange_kernel(n, chunks, x_ref, w_ref, out_ref, buf, part, got, send_sem, recv_sem, part_sem, got_sem, own_sem):
+def partner_of(device, n):
+    quarter = n // 4
+    return (3 - lax.div(device, quarter)) * quarter + lax.rem(device, quarter)
+
+
+def exchange_kernel(n, chunks, x_ref, out_ref, w_ref, buf, part, got, send_sem, recv_sem, part_sem, got_sem, own_sem):
     h = n // 2
     rows_chunk = x_ref.shape[1] // chunks
     depth = h * x_ref.shape[2]
@@ -145,23 +150,27 @@
     half = lax.div(me, h)
     pos = lax.rem(me, h)
     base = half * h
-    other = (1 - half) * h
-    partner = other + pos
+    partner = partner_of(me, n)
+
+    def peer_of(k):
+        quarter = h // 2
+        side = lax.rem(lax.div(pos, quarter) + 1 + lax.div(k, quarter), 2)
+        return side * quarter + lax.rem(pos + k + lax.div(k, quarter), quarter)
 
     barrier = pltpu.get_barrier_semaphore()
 
-    @pl.loop(1, h)
+    @pl.loop(0, h - 1)
     def _(k):
-        pl.semaphore_signal(barrier, inc=1, device_id={"freq": base + lax.rem(pos + k, h)}, device_id_type=pl.DeviceIdType.MESH)
+        pl.semaphore_signal(barrier, inc=1, device_id={"freq": base + peer_of(k)}, device_id_type=pl.DeviceIdType.MESH)
 
     pl.semaphore_signal(barrier, inc=1, device_id={"freq": partner}, device_id_type=pl.DeviceIdType.MESH)
     pl.semaphore_wait(barrier, h)
 
     def bins_copy(s, c, k):
-        p = lax.rem(pos + k, h)
+        p = peer_of(k)
         rows = pl.ds(c * rows_chunk, rows_chunk)
         return pltpu.make_async_remote_copy(
-            src_ref=x_ref.at[(other if s == 0 else base) + p, rows],
+            src_ref=x_ref.at[partner_of(base + p, n) if s == 0 else base + p, rows],
             dst_ref=buf.at[s, rows, pos],
             send_sem=send_sem.at[s, c, k],
             recv_sem=recv_sem.at[s, c, k],
@@ -170,7 +179,7 @@
         )
 
     def own_copy(s):
-        return pltpu.make_async_copy(x_ref.at[(other if s == 0 else base) + pos], buf.at[s, :, pos], own_sem.at[s])
+        return pltpu.make_async_copy(x_ref.at[partner if s == 0 else me], buf.at[s, :, pos], own_sem.at[s])
 
     def sums_copy(c):
         rows = pl.ds(c * rows_chunk, rows_chunk)
@@ -184,12 +193,12 @@
         )
 
     def send_bins(s, c):
-        @pl.loop(1, h)
+        @pl.loop(0, h - 1)
         def _(k):
             bins_copy(s, c, k).start()
 
     def wait_bins(s, c):
-        @pl.loop(1, h)
+        @pl.loop(0, h - 1)
         def _(k):
             bins_copy(s, c, k).wait_recv()
 
@@ -200,6 +209,12 @@
     own_copy(1).start()
     for c in range(chunks):
         send_bins(0, c)
+
+    @pl.loop(0, w_ref.shape[0], step=LAG_ROWS)
+    def _(first):
+        bins = x_ref.shape[2] // 2
+        w_ref[pl.ds(pl.multiple_of(first, LAG_ROWS), LAG_ROWS)] = lag_rows(first, base * bins, bins, (LAG_ROWS, depth))
+
     own_copy(0).wait()
     for c in range(chunks):
         wait_bins(0, c)
@@ -223,22 +238,23 @@
     for c in range(chunks):
         sums_copy(c).wait_send()
         for s in range(2):
-            @pl.loop(1, h)
+            @pl.loop(0, h - 1)
             def _(k):
                 bins_copy(s, c, k).wait_send()
 
 
-def exchange(stacked, weights):
+def exchange(stacked):
     n, recv_local, depth, sources = stacked.shape
-    rows = weights.shape[0]
+    rows = -(-LAGS // LAG_ROWS) * LAG_ROWS
     h = n // 2
-    chunks = math.gcd(recv_local, 4)
+    chunks = math.gcd(recv_local, 8)
     return pl.pallas_call(
         functools.partial(exchange_kernel, n, chunks),
         out_shape=jax.ShapeDtypeStruct((recv_local, LAGS, sources), jnp.float32),
-        in_specs=[pl.BlockSpec(memory_space=pl.ANY), pl.BlockSpec(memory_space=pltpu.VMEM)],
+        in_specs=[pl.BlockSpec(memory_space=pl.ANY)],
         out_specs=pl.BlockSpec(memory_space=pltpu.VMEM),
         scratch_shapes=[
+            pltpu.VMEM((rows, h * depth), jnp.bfloat16),
             pltpu.VMEM((2, recv_local, h, depth, sources), jnp.bfloat16),
             pltpu.VMEM((recv_local, rows, sources), jnp.bfloat16),
             pltpu.VMEM((recv_local, rows, sources), jnp.bfloat16),
@@ -249,7 +265,7 @@
             pltpu.SemaphoreType.DMA((2,)),
         ],
         compiler_params=pltpu.CompilerParams(collective_id=0, has_side_effects=True, vmem_limit_bytes=56 * 1024 * 1024),
-    )(stacked, weights)
+    )(stacked)
 
 
 def local(spectra, valid, ref_spectra, ref_valid):
@@ -279,10 +295,7 @@
         )
         stacked = (stacked / jnp.sqrt(pair_count + 1.0)).astype(jnp.bfloat16)
     stacked = stacked.reshape(freq_devs, recv_local, 2 * local_bins, sources)
-    half_devs = freq_devs // 2
-    first_bin = lax.axis_index("freq") // half_devs * (half_devs * local_bins)
-    weights = half_table(first_bin, local_bins, half_devs, -(-LAGS // 16) * 16)
-    return exchange(stacked, weights).transpose(1, 0, 2)
+    return exchange(stacked).transpose(1, 0, 2)
 
 
 def solution(mesh):

time: 428 us -> 414 us (0.967)
  Pallas kernels: 364 us -> 350 us
  other arithmetic: 16 us -> 4.77 us
  waiting for transfers between devices: 13.6 us -> 21.5 us
    pallas_call x1, Pallas kernels: 318 us -> 304 us  [exchange(): pl.pallas_call(functools.partial(exchange_kernel, n, chunks), out_shape=j...]
    convert_element_type x1 -> x0, other arithmetic: 8.01 us -> none  [half_table(): return values.astype(jnp.bfloat16)]
    ppermute x2, waiting for transfers between devices: 13.6 us -> 21.5 us  [halo_powers(): return (lax.ppermute(last, axis, up), lax.ppermute(first, axis, down))]
  transfers between devices with their start and end apart: 2 -> 2, of which waited for: 2 -> 2; matrix products, arithmetic and copies ran while one was open for 6% -> 4% of each run, Pallas kernels for 0% -> 0%
where the time goes in v3:
time: 414 us; the launch traced here: 410 us
  Pallas kernels  350 us (85%)
  local copies, waits for them, and re-layouts  26.3 us (6%)
  waiting for transfers between devices  21.5 us (5%)
  starting transfers between devices  5.91 us (1%)
  other arithmetic  4.77 us (1%)
    pallas_call x1, Pallas kernels, exchange(): pl.pallas_call(functools.partial(exchange_kernel, n, chunks), out_shape=j...  304 us
    pallas_call x1, Pallas kernels, cross_grams(): pl.pallas_call(gram_kernel, grid=(bins // block,), out_shape=jax.ShapeDty...  46 us
    ppermute x2, waiting for transfers between devices, halo_powers(): return (lax.ppermute(last, axis, up), lax.ppermute(first, axis, down))  21.5 us
    unnamed x14, local copies, waits for them, and re-layouts  13 us
  transfers between devices with their start and end apart: 2, of which 2 were waited for; matrix products, arithmetic and copies ran while one was open for 4% of the time, Pallas kernels for 0%

profile of v3, /device:TPU:15, one launch (start us, length us, event | category | flops | bytes accessed | tf_op | source)
XLA Modules:
  0.0 410.5 jit_solution(7805523023855878582)
XLA Ops:
  0.0 2.7 fusion.12
  2.7 0.0 slice-start.1
  2.8 0.5 convert_bitcast_fusion.2
  3.3 0.1 fusion.8
  3.4 0.9 slice-done.1
  4.4 2.8 fusion.11
  7.1 1.2 convert_bitcast_fusion
  8.4 0.5 fusion.3
  8.9 0.2 pad_maximum_fusion
  9.1 3.7 collective-permute-start
  12.8 0.1 fusion.6
  12.9 0.5 fusion.1
  13.4 0.2 pad_maximum_fusion.1
  13.7 2.2 collective-permute-start.1
  15.9 4.2 %copy.23 = bf16[96,32,2,256]{3,0,2,1:T(8,128)(2,1)} copy(bf16[96,32,2,256]{3,2,1,0:T(2,128)(2,1)S(1)} %copy-done) | data formatting | bytes 6291456 | tf_op args[2]
  20.1 7.8 %copy.22 = bf16[96,32,2,512]{3,0,2,1:T(8,128)(2,1)} copy(bf16[96,32,2,512]{3,2,1,0:T(2,128)(2,1)S(1)} %bitcast.28) | data formatting | bytes 12582912 | tf_op args[0]
  28.0 0.7 convert_element_type.39.ref_valid_ref
  28.6 0.7 convert_element_type.38.valid_ref
  29.3 1.5 fusion.4.scale_ref
  30.8 14.2 %collective-permute-done.before_ref = f32[10,96,768]{2,1,0:T(8,128)S(1)} collective-permute-done((f32[10,96,768]{2,1,0:T(8,128)S(1)}, f32[10,96,768]{2,1,0:T(8,128)S(1)}, u32[]{:S(2)}, u32[]{:S(2)}) %collective-permute-start) | collective-permute-done | bytes 2949152 | tf_op jit(solution)/shard_map/ppermute | solution.py:35
  44.9 7.3 %collective-permute-done.1.after_ref = f32[10,96,768]{2,1,0:T(8,128)} collective-permute-done((f32[10,96,768]{2,1,0:T(8,128)S(1)}, f32[10,96,768]{2,1,0:T(8,128)}, u32[]{:S(2)}, u32[]{:S(2)}) %collective-permute-start.1) | collective-permute-done | bytes 2949152 | tf_op jit(solution)/shard_map/ppermute | solution.py:35
  52.3 46.0 %shard_map.46 = bf16[512,2,32,256]{3,2,1,0:T(8,128)(2,1)} custom-call(bf16[32,2,96,512]{3,2,1,0:T(8,128)(2,1)} %bitcast.26, bf16[32,2,96,256]{3,2,1,0:T(8,128)(2,1)} %bitcast.29, f32[10,96,768]{2,1,0:T(8,128)} %copy-done.1, f32[10,96,768]{2,1,0:T(8,128)} %collective-permute-done.1.after_ref, f32[96,512]{1,0:T(8,128)} %convert_element_type.38.valid_ref, ...), custom_call_target="tpu_custom_call" | custom-call | tf_op jit(solution)/shard_map/pallas_call | solution.py:105
  98.3 304.4 %shard_map.47 = f32[16,401,256]{2,1,0:T(8,128)} custom-call(bf16[32,16,64,256]{3,2,1,0:T(8,128)(2,1)} %bitcast.24), custom_call_target="tpu_custom_call" | custom-call | tf_op jit(solution)/shard_map/pallas_call | solution.py:251
  402.7 7.8 %copy.11 = f32[401,16,256]{2,1,0:T(8,128)} copy(f32[401,16,256]{2,0,1:T(8,128)} %bitcast.25) | data formatting | bytes 13139968 | tf_op jit(solution)/shard_map/transpose | solution.py:298
  (11 shorter events, 0.0 us)
Async XLA Ops:
  0.0 3.4 slice-start
  2.7 1.6 slice-start.1
  9.1 35.8 %collective-permute-start = (f32[10,96,768]{2,1,0:T(8,128)S(1)}, f32[10,96,768]{2,1,0:T(8,128)S(1)}, u32[]{:S(2)}, u32[]{:S(2)}) collective-permute-start(f32[10,96,768]{2,1,0:T(8,128)S(1)} %pad_maximum_fusion), channel_id=1, source_target_pairs={{0,1},{1,2},{2,3},{3,4},{4,5},{5,6},{6,7},{7,8},{8,9},{9,10},{10,1... | collective-permute-start | bytes 8847368 | tf_op jit(solution)/shard_map/ppermute | solution.py:35
  13.4 2.5 copy-start
  13.7 38.6 %collective-permute-start.1 = (f32[10,96,768]{2,1,0:T(8,128)S(1)}, f32[10,96,768]{2,1,0:T(8,128)}, u32[]{:S(2)}, u32[]{:S(2)}) collective-permute-start(f32[10,96,768]{2,1,0:T(8,128)S(1)} %pad_maximum_fusion.1), channel_id=1, source_target_pairs={{1,0},{2,1},{3,2},{4,3},{5,4},{6,5},{7,6},{8,7},{9,8},{10,9},{11,1... | collective-permute-start | bytes 8847368 | tf_op jit(solution)/shard_map/ppermute | solution.py:35
  20.1 7.8 %copy-start.3 = (s32[96,256]{1,0:T(8,128)S(1)}, s32[96,256]{1,0:T(8,128)}, u32[]{:S(2)}) copy-start(s32[96,256]{1,0:T(8,128)} %param.7) | copy-start | bytes 294916
  20.1 8.5 %copy-start.2 = (s32[96,512]{1,0:T(8,128)S(1)}, s32[96,512]{1,0:T(8,128)}, u32[]{:S(2)}) copy-start(s32[96,512]{1,0:T(8,128)} %param.5) | copy-start | bytes 589828
  44.9 7.4 %copy-start.1 = (f32[10,96,768]{2,1,0:T(8,128)}, f32[10,96,768]{2,1,0:T(8,128)S(1)}, u32[]{:S(2)}) copy-start(f32[10,96,768]{2,1,0:T(8,128)S(1)} %collective-permute-done.before_ref) | copy-start | bytes 8847364

commit v4 on v3

--- a/solution.py
+++ b/solution.py
@@ -247,7 +247,7 @@
     n, recv_local, depth, sources = stacked.shape
     rows = -(-LAGS // LAG_ROWS) * LAG_ROWS
     h = n // 2
-    chunks = math.gcd(recv_local, 8)
+    chunks = math.gcd(recv_local, 4)
     return pl.pallas_call(
         functools.partial(exchange_kernel, n, chunks),
         out_shape=jax.ShapeDtypeStruct((recv_local, LAGS, sources), jnp.float32),

time: 414 us -> 405 us (0.978)
  Pallas kernels: 350 us -> 345 us
    pallas_call x1, Pallas kernels: 304 us -> 299 us  [exchange(): pl.pallas_call(functools.partial(exchange_kernel, n, chunks), out_shape=j...]
where the time goes in v4:
time: 405 us
  Pallas kernels  345 us (85%)
  local copies, waits for them, and re-layouts  26.3 us (6%)
  waiting for transfers between devices  21.5 us (5%)
  starting transfers between devices  5.91 us (1%)
  other arithmetic  4.77 us (1%)
    pallas_call x1, Pallas kernels, exchange(): pl.pallas_call(functools.partial(exchange_kernel, n, chunks), out_shape=j...  299 us
    pallas_call x1, Pallas kernels, cross_grams(): pl.pallas_call(gram_kernel, grid=(bins // block,), out_shape=jax.ShapeDty...  46 us
    ppermute x2, waiting for transfers between devices, halo_powers(): return (lax.ppermute(last, axis, up), lax.ppermute(first, axis, down))  21.5 us
    unnamed x14, local copies, waits for them, and re-layouts  13 us
  transfers between devices with their start and end apart: 2, of which 2 were waited for; matrix products, arithmetic and copies ran while one was open for 4% of the time, Pallas kernels for 0%

profile of v4, /device:TPU:15, one launch (start us, length us, event | category | flops | bytes accessed | tf_op | source)
XLA Modules:
  0.0 404.7 jit_solution(6849255693419219133)
XLA Ops:
  0.0 2.7 fusion.12
  2.7 0.0 slice-start.1
  2.8 0.5 convert_bitcast_fusion.2
  3.3 0.1 fusion.8
  3.4 0.9 slice-done.1
  4.4 2.8 fusion.11
  7.1 1.2 convert_bitcast_fusion
  8.4 0.5 fusion.3
  8.9 0.2 pad_maximum_fusion
  9.1 3.7 collective-permute-start
  12.8 0.1 fusion.6
  12.9 0.5 fusion.1
  13.4 0.2 pad_maximum_fusion.1
  13.7 2.2 collective-permute-start.1
  15.9 4.2 %copy.23 = bf16[96,32,2,256]{3,0,2,1:T(8,128)(2,1)} copy(bf16[96,32,2,256]{3,2,1,0:T(2,128)(2,1)S(1)} %copy-done) | data formatting | bytes 6291456 | tf_op args[2]
  20.1 7.8 %copy.22 = bf16[96,32,2,512]{3,0,2,1:T(8,128)(2,1)} copy(bf16[96,32,2,512]{3,2,1,0:T(2,128)(2,1)S(1)} %bitcast.28) | data formatting | bytes 12582912 | tf_op args[0]
  28.0 0.7 convert_element_type.39.ref_valid_ref
  28.6 0.7 convert_element_type.38.valid_ref
  29.3 1.5 fusion.4.scale_ref
  30.8 14.2 %collective-permute-done.before_ref = f32[10,96,768]{2,1,0:T(8,128)S(1)} collective-permute-done((f32[10,96,768]{2,1,0:T(8,128)S(1)}, f32[10,96,768]{2,1,0:T(8,128)S(1)}, u32[]{:S(2)}, u32[]{:S(2)}) %collective-permute-start) | collective-permute-done | bytes 2949152 | tf_op jit(solution)/shard_map/ppermute | solution.py:35
  44.9 7.3 %collective-permute-done.1.after_ref = f32[10,96,768]{2,1,0:T(8,128)} collective-permute-done((f32[10,96,768]{2,1,0:T(8,128)S(1)}, f32[10,96,768]{2,1,0:T(8,128)}, u32[]{:S(2)}, u32[]{:S(2)}) %collective-permute-start.1) | collective-permute-done | bytes 2949152 | tf_op jit(solution)/shard_map/ppermute | solution.py:35
  52.3 46.0 %shard_map.46 = bf16[512,2,32,256]{3,2,1,0:T(8,128)(2,1)} custom-call(bf16[32,2,96,512]{3,2,1,0:T(8,128)(2,1)} %bitcast.26, bf16[32,2,96,256]{3,2,1,0:T(8,128)(2,1)} %bitcast.29, f32[10,96,768]{2,1,0:T(8,128)} %copy-done.1, f32[10,96,768]{2,1,0:T(8,128)} %collective-permute-done.1.after_ref, f32[96,512]{1,0:T(8,128)} %convert_element_type.38.valid_ref, ...), custom_call_target="tpu_custom_call" | custom-call | tf_op jit(solution)/shard_map/pallas_call | solution.py:105
  98.3 298.6 %shard_map.47 = f32[16,401,256]{2,1,0:T(8,128)} custom-call(bf16[32,16,64,256]{3,2,1,0:T(8,128)(2,1)} %bitcast.24), custom_call_target="tpu_custom_call" | custom-call | tf_op jit(solution)/shard_map/pallas_call | solution.py:251
  396.9 7.8 %copy.11 = f32[401,16,256]{2,1,0:T(8,128)} copy(f32[401,16,256]{2,0,1:T(8,128)} %bitcast.25) | data formatting | bytes 13139968 | tf_op jit(solution)/shard_map/transpose | solution.py:298
  (11 shorter events, 0.0 us)
Async XLA Ops:
  0.0 3.4 slice-start
  2.7 1.6 slice-start.1
  9.1 35.8 %collective-permute-start = (f32[10,96,768]{2,1,0:T(8,128)S(1)}, f32[10,96,768]{2,1,0:T(8,128)S(1)}, u32[]{:S(2)}, u32[]{:S(2)}) collective-permute-start(f32[10,96,768]{2,1,0:T(8,128)S(1)} %pad_maximum_fusion), channel_id=1, source_target_pairs={{0,1},{1,2},{2,3},{3,4},{4,5},{5,6},{6,7},{7,8},{8,9},{9,10},{10,1... | collective-permute-start | bytes 8847368 | tf_op jit(solution)/shard_map/ppermute | solution.py:35
  13.4 2.5 copy-start
  13.7 38.6 %collective-permute-start.1 = (f32[10,96,768]{2,1,0:T(8,128)S(1)}, f32[10,96,768]{2,1,0:T(8,128)}, u32[]{:S(2)}, u32[]{:S(2)}) collective-permute-start(f32[10,96,768]{2,1,0:T(8,128)S(1)} %pad_maximum_fusion.1), channel_id=1, source_target_pairs={{1,0},{2,1},{3,2},{4,3},{5,4},{6,5},{7,6},{8,7},{9,8},{10,9},{11,1... | collective-permute-start | bytes 8847368 | tf_op jit(solution)/shard_map/ppermute | solution.py:35
  20.1 7.8 %copy-start.3 = (s32[96,256]{1,0:T(8,128)S(1)}, s32[96,256]{1,0:T(8,128)}, u32[]{:S(2)}) copy-start(s32[96,256]{1,0:T(8,128)} %param.7) | copy-start | bytes 294916
  20.1 8.5 %copy-start.2 = (s32[96,512]{1,0:T(8,128)S(1)}, s32[96,512]{1,0:T(8,128)}, u32[]{:S(2)}) copy-start(s32[96,512]{1,0:T(8,128)} %param.5) | copy-start | bytes 589828
  44.9 7.4 %copy-start.1 = (f32[10,96,768]{2,1,0:T(8,128)}, f32[10,96,768]{2,1,0:T(8,128)S(1)}, u32[]{:S(2)}) copy-start(f32[10,96,768]{2,1,0:T(8,128)S(1)} %collective-permute-done.before_ref) | copy-start | bytes 8847364
